TPU v7x, 32 devices: a whole 2x2x4 slice. The times are simulated.
32 devices in a mesh: head: 4 (over y, core), seq: 8 (over z, x).
Axes of the slice: x: 2, y: 2, z: 4, core: 2. Of those that a mesh axis runs over, the one named last changes fastest.
Arguments:
- queries: bfloat16 [4096, 4096], P('seq', 'head'), may hold values from -6 to 6
- keys: bfloat16 [4096, 4096], P('seq', 'head'), may hold values from -6 to 6
- values: bfloat16 [4096, 4096], P('seq', 'head'), may hold values from -6 to 6
- rate: float32 [8, 4096], P('head', 'seq'), may hold values from 0.0001 to 0.001
- fast_gate: float32 [8, 512, 512], P('head', 'seq'), may hold values from -3 to 3
- fast_up: float32 [8, 512, 512], P('head', 'seq'), may hold values from -3 to 3
- fast_down: float32 [8, 512, 512], P('head', 'seq'), may hold values from -8 to 8
- out_gain: float32 [4096], P('head'), may hold values from 0.25 to 1.75
Outputs:
- mixed: bfloat16 [4096, 4096], P('seq', 'head')
- new_gate: float32 [8, 512, 512], P('head', 'seq')
- new_up: float32 [8, 512, 512], P('head', 'seq')
- new_down: float32 [8, 512, 512], P('head', 'seq')
All inputs are finite; a program needn't handle non-finite values.
Results may differ from a plain program's by a relative error of at most 0.012.
Values may be sent and summed in bfloat16 or wider, within the bound.
A program may use at most 128 MiB of HBM per device.

v0:
```python
import math

import jax
import jax.numpy as jnp
from jax import lax
from jax.sharding import PartitionSpec as P

HEADS = 8
HD = 512
WINDOW = 512


EPS = 1e-06


def from_behind(block, axis, distance):
    devices = range(lax.axis_size(axis))
    route = [(i - distance, i) for i in devices if i - distance in devices]
    return lax.ppermute(block, axis, route)


def column_sq(matrix):
    return jnp.sum(matrix * matrix, axis=1)


def apply_ratio(upd, old_sq, new_sq):
    return upd * (jnp.sqrt(old_sq) / jnp.sqrt(new_sq + EPS))[:, None, :]


def gradients(k_three, scaled, w_oneb, w_threeb, w_twob):
    pre_a = jnp.einsum("thd,hdf->thf", k_three, w_oneb, preferred_element_type=jnp.float32)
    pre_b = jnp.einsum("thd,hdf->thf", k_three, w_threeb, preferred_element_type=jnp.float32)
    sigma = jax.nn.sigmoid(pre_a)
    hidden = (pre_a * sigma * pre_b).astype(jnp.bfloat16)
    grad_two = jnp.einsum("thf,thd->hfd", hidden, scaled, preferred_element_type=jnp.float32)
    back = jnp.einsum("thd,hfd->thf", scaled, w_twob, preferred_element_type=jnp.float32)
    d_gate = (back * pre_b * sigma * (1.0 + pre_a * (1.0 - sigma))).astype(jnp.bfloat16)
    d_up = (back * pre_a * sigma).astype(jnp.bfloat16)
    grad_one = jnp.einsum("thd,thf->hdf", k_three, d_gate, preferred_element_type=jnp.float32)
    grad_three = jnp.einsum("thd,thf->hdf", k_three, d_up, preferred_element_type=jnp.float32)
    return (grad_one, grad_three, grad_two)


def local(queries, keys, values, rate, fast_gate, fast_up, fast_down, out_gain):
    rows, width = queries.shape
    heads = fast_gate.shape[0]
    head_dim = width // heads
    seq_pos = lax.axis_index("seq")
    q_three = queries.reshape(rows, heads, head_dim)
    k_three = keys.reshape(rows, heads, head_dim)
    v_three = values.reshape(rows, heads, head_dim)
    prev_k, prev_v = from_behind((keys, values), "seq", 1)
    blocks = rows // WINDOW
    ext_k = jnp.concatenate([prev_k, keys], axis=0).reshape(blocks + 1, WINDOW, heads, head_dim)
    ext_v = jnp.concatenate([prev_v, values], axis=0).reshape(blocks + 1, WINDOW, heads, head_dim)
    k_win = jnp.concatenate([ext_k[:-1], ext_k[1:]], axis=1)
    v_win = jnp.concatenate([ext_v[:-1], ext_v[1:]], axis=1)
    q_blocks = q_three.reshape(blocks, WINDOW, heads, head_dim)
    scores = jnp.einsum("bqhd,bkhd->bhqk", q_blocks, k_win, preferred_element_type=jnp.float32)
    scores = scores * (1.0 / math.sqrt(head_dim))
    rows_i = jnp.arange(WINDOW, dtype=jnp.int32)[None, :, None]
    cols_j = jnp.arange(2 * WINDOW, dtype=jnp.int32)[None, None, :]
    block_at = jnp.arange(blocks, dtype=jnp.int32)[:, None, None] * WINDOW
    valid = (
        (cols_j > rows_i)
        & (cols_j <= rows_i + WINDOW)
        & (block_at + cols_j + seq_pos * rows >= WINDOW)
    )
    scores = jnp.where(valid[:, None], scores, -jnp.inf)
    top = jnp.max(scores, axis=-1, keepdims=True)
    expo = jnp.exp(scores - top)
    probs = (expo / jnp.sum(expo, axis=-1, keepdims=True)).astype(jnp.bfloat16)
    attn = jnp.einsum("bhqk,bkhd->bqhd", probs, v_win, preferred_element_type=jnp.float32)
    attn = attn.reshape(rows, heads, head_dim)
    scaled = (rate.T[:, :, None] * v_three.astype(jnp.float32)).astype(jnp.bfloat16)
    full_one, full_three, full_two = (
        lax.all_gather(fast_gate, "seq", axis=1, tiled=True),
        lax.all_gather(fast_up, "seq", axis=1, tiled=True),
        lax.all_gather(fast_down, "seq", axis=1, tiled=True),
    )
    grad_one, grad_three, grad_two = gradients(
        k_three,
        scaled,
        full_one.astype(jnp.bfloat16),
        full_three.astype(jnp.bfloat16),
        full_two.astype(jnp.bfloat16),
    )
    grad_one, grad_three, grad_two = lax.psum((grad_one, grad_three, grad_two), "seq")
    upd_one = full_one + grad_one
    upd_three = full_three + grad_three
    upd_two = full_two + grad_two
    whole_one = apply_ratio(upd_one, column_sq(full_one), column_sq(upd_one))
    whole_three = apply_ratio(upd_three, column_sq(full_three), column_sq(upd_three))
    whole_two = apply_ratio(upd_two, column_sq(full_two), column_sq(upd_two))
    use_one = whole_one.astype(jnp.bfloat16)
    use_three = whole_three.astype(jnp.bfloat16)
    use_two = whole_two.astype(jnp.bfloat16)
    shard = fast_gate.shape[1]
    first = seq_pos * shard
    new_gate = lax.dynamic_slice_in_dim(whole_one, first, shard, 1)
    new_up = lax.dynamic_slice_in_dim(whole_three, first, shard, 1)
    new_down = lax.dynamic_slice_in_dim(whole_two, first, fast_down.shape[1], 1)
    apply_a = jnp.einsum("thd,hdf->thf", q_three, use_one, preferred_element_type=jnp.float32)
    apply_b = jnp.einsum("thd,hdf->thf", q_three, use_three, preferred_element_type=jnp.float32)
    apply_h = (apply_a * jax.nn.sigmoid(apply_a) * apply_b).astype(jnp.bfloat16)
    branch = jnp.einsum("thf,hfd->thd", apply_h, use_two, preferred_element_type=jnp.float32)
    local_sq = jnp.sum(branch * branch, axis=(1, 2))
    total_sq = lax.psum(local_sq, "head")
    inv = lax.rsqrt(total_sq / (HEADS * HD) + EPS)
    gain = out_gain.reshape(heads, head_dim)
    mixed = (attn + branch * inv[:, None, None] * gain[None]).astype(jnp.bfloat16)
    return (mixed.reshape(rows, width), new_gate, new_up, new_down)


def solution(mesh):
    in_specs = (
        P("seq", "head"),
        P("seq", "head"),
        P("seq", "head"),
        P("head", "seq"),
        P("head", "seq", None),
        P("head", "seq", None),
        P("head", "seq", None),
        P("head"),
    )
    out_specs = (
        P("seq", "head"),
        P("head", "seq", None),
        P("head", "seq", None),
        P("head", "seq", None),
    )
    return jax.shard_map(local, mesh=mesh, in_specs=in_specs, out_specs=out_specs, check_vma=False)
```

profile of v0, /device:TPU:0, one launch (start us, length us, event | category | flops | bytes accessed | tf_op | source)
XLA Modules:
  0.0 459.4 jit_solution(2337113670307311692)
XLA Ops:
  7.2 1.9 copy.60
  9.2 1.9 copy.63
  11.2 0.7 all-gather.4.cloned.1.call-update
  11.9 1.6 convert_element_type.61
  13.5 49.0 %all-gather.6.cloned.1.call-done = f32[2,512,512]{2,0,1:T(2,128)} async-done(((f32[2,64,512]{2,0,1:T(2,128)}), f32[2,512,512]{2,0,1:T(2,128)}) %all-gather.6.cloned.1.call-update) | async-done | bytes 2097168 | tf_op jit(solution)/shard_map/all_gather | solution.py:77
  62.5 2.7 copy.61
  65.3 47.6 %all-gather.8.cloned.1.call-done = f32[2,512,512]{2,0,1:T(2,128)} async-done(((f32[2,64,512]{2,0,1:T(2,128)}), f32[2,512,512]{2,0,1:T(2,128)}) %all-gather.8.cloned.1.call-update) | async-done | bytes 2097168 | tf_op jit(solution)/shard_map/all_gather | solution.py:78
  112.9 4.1 copy.64
  117.0 0.7 fusion.34
  117.7 0.8 copy-done
  118.6 0.8 fusion.32
  119.4 0.5 copy-done.10
  119.9 0.9 copy-done.12
  120.7 1.0 copy-done.5
  121.7 2.1 fusion.52
  123.8 38.8 %all-gather.4.cloned.1.call-done = f32[2,512,512]{2,1,0:T(8,128)} async-done(((f32[2,64,512]{2,1,0:T(8,128)}), f32[2,512,512]{2,1,0:T(8,128)}) %all-gather.4.cloned.1.call-update) | async-done | bytes 2097168 | tf_op jit(solution)/shard_map/all_gather | solution.py:79
  162.7 3.2 fusion.44
  165.9 0.3 copy-done.13
  166.2 2.6 convolution_bitcast_fusion.1
  168.8 2.1 convolution_bitcast_fusion
  170.9 1.3 copy.54
  172.2 3.6 collective-permute-start.1
  175.8 4.4 collective-permute-start
  180.1 2.3 copy.53
  182.5 1.3 copy.57
  183.8 1.2 fusion.27
  185.1 25.3 %collective-permute-done.1 = bf16[512,1024]{0,1:T(8,128)(2,1)} collective-permute-done((bf16[512,1024]{0,1:T(8,128)(2,1)}, bf16[512,1024]{0,1:T(8,128)(2,1)}, u32[]{:S(2)}, u32[]{:S(2)}) %collective-permute-start.1) | collective-permute-done | bytes 1048608 | tf_op jit(solution)/shard_map/ppermute | solution.py:19
  210.4 2.4 copy.56
  212.8 27.8 %collective-permute-done = bf16[512,1024]{1,0:T(8,128)(2,1)} collective-permute-done((bf16[512,1024]{1,0:T(8,128)(2,1)}, bf16[512,1024]{1,0:T(8,128)(2,1)}, u32[]{:S(2)}, u32[]{:S(2)}) %collective-permute-start) | collective-permute-done | bytes 1048608 | tf_op jit(solution)/shard_map/ppermute | solution.py:19
  240.5 2.3 copy.52
  242.8 2.9 fusion.6
  245.8 4.0 fusion.72
  249.8 0.9 multiply_reduce_fusion.2
  250.7 0.7 copy-done.2
  251.5 0.9 multiply_reduce_fusion.4
  252.4 172.0 %all-reduce.3.cloned.1.call-done = (f32[2,512,512]{1,2,0:T(8,128)}, f32[2,512,512]{1,2,0:T(8,128)}, f32[2,512,512]{2,1,0:T(8,128)}) async-done(((f32[2,512,512]{1,2,0:T(8,128)}, f32[2,512,512]{1,2,0:T(8,128)}, f32[2,512,512]{2,1,0:T(8,128)}), (f32[2,512,512]{1,2,0:T(8,128)}, f32[2,512,512]{1,2,0:T(8,128)}, f32[2,512,512]{2,1,0:T(8,128)})) %all-reduce.3.cloned.1.call-update) | async-done | bytes 6291472 | tf_op jit(solution)/shard_map/psum | solution.py:88
  424.4 3.4 multiply_reduce_fusion.1
  428.0 2.1 fusion.38
  430.4 0.6 copy-done.9
  431.0 0.5 multiply_reduce_fusion.5
  431.8 0.8 constant_dynamic-slice_fusion
  432.9 0.4 copy-done.8
  433.5 5.4 %multiply_reduce_fusion = (f32[512]{0:T(512)S(1)}, f32[2,512,512]{2,1,0:T(8,128)}) fusion(f32[2,512,512]{2,1,0:T(8,128)} %fusion.38, f32[2,512,512]{1,2,0:T(8,128)S(1)} %broadcast_multiply_fusion, bf16[64,2,8,512]{3,2,1,0:T(8,128)(2,1)} %bitcast.147, f32[2,512,512]{2,1,0:T(8,128)} %copy-done.8), kind=kOutput, calls=%fused_computation.40 | convolution fusion | flops 1078984192 | bytes 9439232 | tf_op jit(solution)/shard_map/thf,hfd->thd/dot_general | solution.py:106
  438.9 6.2 %psum.31 = f32[512]{0:T(512)S(1)} all-reduce(f32[512]{0:T(512)S(1)} %get-tuple-element.28), channel_id=1, replica_groups=mesh['head'=4,'seq'=8] {'head'}, use_global_device_ids=true, to_apply=%region_12.13 | all-reduce | flops 512 | bytes 4096 | tf_op jit(solution)/shard_map/psum | solution.py:108
  445.1 4.7 %fusion.9 = bf16[512,2,512]{0,2,1:T(8,128)(2,1)S(1)} fusion(f32[2,512,512]{2,1,0:T(8,128)} %get-tuple-element.29, f32[2,512,1024]{1,2,0:T(8,128)} %get-tuple-element.27, f32[2,512]{1,0:T(2,128)S(1)} %get-tuple-element.26, bf16[1,512,2,512]{1,3,2,0:T(8,128)(2,1)} %bitcast.150, bf16[1,512,2,512]{1,3,2,0:T(8,128)(2,1)} %bitcast.151, f32[2,512]{1,0:T(2,128)S(1)} %mul.153, ...), kind=kOutput, calls=%fused_computation.16 | convolution fusion | flops 1082130432 | bytes 9447424 | tf_op jit(solution)/shard_map/bhqk,bkhd->bqhd/dot_general | solution.py:73
  449.8 1.3 copy.76
  451.1 0.9 copy.78
  452.0 0.9 copy.77
  (47 shorter events, 1.4 us)
Async XLA Ops:
  7.2 4.7 %copy-start.6 = (bf16[512,1024]{1,0:T(8,128)(2,1)S(1)}, bf16[512,1024]{1,0:T(8,128)(2,1)}, u32[]{:S(2)}) copy-start(bf16[512,1024]{1,0:T(8,128)(2,1)} %param.10) | copy-start | bytes 3145732
  7.2 55.3 %all-gather.6.cloned.1.call-start = ((), (), s32[]{:S(2)}) async-start(), calls=%async_computation.1 | async-start | bytes 2359296 | tf_op jit(solution)/shard_map/all_gather | solution.py:77
  9.2 103.7 %all-gather.8.cloned.1.call-start = ((), (), s32[]{:S(2)}) async-start(), calls=%async_computation.2 | async-start | bytes 2359296 | tf_op jit(solution)/shard_map/all_gather | solution.py:78
  11.1 151.6 %all-gather.4.cloned.1.call-start = ((), (), s32[]{:S(2)}) async-start(), calls=%async_computation | async-start | bytes 2359296 | tf_op jit(solution)/shard_map/all_gather | solution.py:79
  11.9 412.6 %all-reduce.3.cloned.1.call-start = ((), (), s32[]{:S(2)}) async-start(), calls=%async_computation.3 | async-start | bytes 12582912 | tf_op jit(solution)/shard_map/psum | solution.py:88
  65.3 51.7 %copy-start.1 = (bf16[512,1024]{1,0:T(8,128)(2,1)S(1)}, bf16[512,1024]{1,0:T(8,128)(2,1)}, u32[]{:S(2)}) copy-start(bf16[512,1024]{1,0:T(8,128)(2,1)} %param.9) | copy-start | bytes 3145732
  117.0 1.6 copy-start
  118.6 1.3 copy-start.10
  118.6 3.1 copy-start.5
  118.6 3.1 copy-start.17
  119.4 1.4 copy-start.12
  162.7 3.2 copy-start.11
  162.7 3.5 copy-start.13
  172.2 10.2 %copy-start.7 = (bf16[512,1024]{0,1:T(8,128)(2,1)S(1)}, bf16[512,1024]{0,1:T(8,128)(2,1)}, u32[]{:S(2)}) copy-start(bf16[512,1024]{0,1:T(8,128)(2,1)} %copy.54) | copy-start | bytes 3145732
  172.2 38.2 %collective-permute-start.1 = (bf16[512,1024]{0,1:T(8,128)(2,1)}, bf16[512,1024]{0,1:T(8,128)(2,1)}, u32[]{:S(2)}, u32[]{:S(2)}) collective-permute-start(bf16[512,1024]{0,1:T(8,128)(2,1)} %copy.54), channel_id=1, source_target_pairs={{0,1},{1,2},{2,3},{3,4},{4,5},{5,6},{6,7},{8,9},{9,10},{10,11},{11... | collective-permute-start | bytes 3145736 | tf_op jit(solution)/shard_map/ppermute | solution.py:19
  175.8 64.8 %collective-permute-start = (bf16[512,1024]{1,0:T(8,128)(2,1)}, bf16[512,1024]{1,0:T(8,128)(2,1)}, u32[]{:S(2)}, u32[]{:S(2)}) collective-permute-start(bf16[512,1024]{1,0:T(8,128)(2,1)} %param.10), channel_id=1, source_target_pairs={{0,1},{1,2},{2,3},{3,4},{4,5},{5,6},{6,7},{8,9},{9,10},{10,11},{11... | collective-permute-start | bytes 3145736 | tf_op jit(solution)/shard_map/ppermute | solution.py:19
  180.1 3.7 copy-start.16
  210.4 32.4 %copy-start.14 = (bf16[512,1024]{1,0:T(8,128)(2,1)S(1)}, bf16[512,1024]{1,0:T(8,128)(2,1)}, u32[]{:S(2)}) copy-start(bf16[512,1024]{1,0:T(8,128)(2,1)} %param.8) | copy-start | bytes 3145732
  242.8 2.9 copy-start.15
  245.7 4.1 copy-start.3
  249.8 1.7 copy-start.2
  428.0 2.3 copy-start.4
  428.0 3.0 copy-start.9
  431.8 1.5 copy-start.8
Sparse Core Ops, SparseCore 0:
  10.7 51.7 all-gather.5
  65.2 47.6 all-gather.7
  115.1 47.5 all-gather.3
  171.0 253.3 all-reduce.2
where the time goes:
time: 460 us; the launch traced here: 459 us
  waiting for transfers between devices  361 us (78%)
  local copies, waits for them, and re-layouts  29.8 us (6%)
  matrix products  26.7 us (6%)
  between operations  14 us (3%)
  other arithmetic  13.4 us (3%)
  starting transfers between devices  8.08 us (2%)
  blocking collectives  6.21 us (1%)
    psum x1, waiting for transfers between devices, local(): lax.psum((grad_one, grad_three, grad_two), 'seq')  172 us
    ppermute x2, waiting for transfers between devices, from_behind(): return lax.ppermute(block, axis, route)  53.1 us
    all_gather x1, waiting for transfers between devices, local(): lax.all_gather(fast_gate, 'seq', axis=1, tiled=True)  49 us
    all_gather x1, waiting for transfers between devices, local(): lax.all_gather(fast_up, 'seq', axis=1, tiled=True)  47.6 us
    all_gather x1, waiting for transfers between devices, local(): lax.all_gather(fast_down, 'seq', axis=1, tiled=True)  38.8 us
    unnamed x43, local copies, waits for them, and re-layouts  15.8 us
  transfers between devices with their start and end apart: 6, of which 6 were waited for; matrix products, arithmetic and copies ran while one was open for 7% of the time, Pallas kernels for 0%

commit v1 on v0

v1 whole, which is shorter than its diff:
```python
import functools
import math

import jax
import jax.numpy as jnp
from jax import lax
from jax.experimental import pallas as pl
from jax.experimental.pallas import tpu as pltpu
from jax.sharding import PartitionSpec as P

WINDOW = 512
EPS = 1e-06
TILE = 128
MESH = pl.DeviceIdType.MESH
F32 = jnp.float32
BF16 = jnp.bfloat16


def dot(a, b):
    return jnp.dot(a, b, preferred_element_type=F32)


def dot_lhs_t(a, b):
    return lax.dot_general(a, b, (((0,), (0,)), ((), ())), preferred_element_type=F32)


def dot_rhs_t(a, b):
    return lax.dot_general(a, b, (((1,), (1,)), ((), ())), preferred_element_type=F32)


def kernel(
    n, hn,
    q, k, v, rate, gain, w1, w3, w2,
    mixed, o1, o3, o2,
    wg, ug, pg, rs_out, rs_in, own, kx, vx, gv, hid, dab, attn, branch, sq, sq_in,
    ag_s, ag_r, rs_s, rs_r, au_s, au_r, halo_s, halo_r, sq_s, sq_r,
):
    rows, width = q.shape
    heads, shard, hd = w1.shape
    fast = w1.shape[2]
    half = n // 2
    me = lax.axis_index("seq")
    hme = lax.axis_index("head")
    odd = lax.rem(me, 2)
    pos = (1 - odd) * lax.div(me, 2) + odd * (n - lax.div(me + 1, 2))

    def at_pos(p):
        p = lax.rem(p + 2 * n, n)
        back = lax.div(p, half)
        return (1 - back) * 2 * p + back * (2 * (n - p) - 1)

    neighbour = (at_pos(pos + 1), at_pos(pos - 1))
    sign = (1, -1)
    after, before = lax.rem(me + 1, n), lax.rem(me + n - 1, n)

    barrier = pltpu.get_barrier_semaphore()
    for s in (neighbour[0], neighbour[1], after, before):
        pl.semaphore_signal(barrier, inc=1, device_id={"seq": s}, device_id_type=MESH)
    for d in range(1, hn):
        pl.semaphore_signal(
            barrier, inc=1, device_id={"head": lax.rem(hme + d, hn)}, device_id_type=MESH
        )
    for h in range(heads):
        for m, w in enumerate((w1, w3, w2)):
            wg[h, me, m] = w[h].astype(BF16)
    pl.semaphore_wait(barrier, 4 + hn - 1)

    sent = []

    def carries(h, d):
        return h % 2 == d

    def gather_send(buf, ss, rr, h, s):
        for d in range(2):
            if s == half and not carries(h, d):
                continue
            owner = at_pos(pos - sign[d] * (s - 1))
            if s > 1:
                gather_wait(buf, ss, rr, h, s - 1, d)
            block = buf.at[h, owner]
            c = pltpu.make_async_remote_copy(
                src_ref=block, dst_ref=block,
                send_sem=ss.at[d, h, s - 1], recv_sem=rr.at[d, h, s - 1],
                device_id={"seq": neighbour[d]}, device_id_type=MESH,
            )
            c.start()
            sent.append(c)

    def gather_wait(buf, ss, rr, h, s, d):
        owner = at_pos(pos - sign[d] * s)
        block = buf.at[h, owner]
        pltpu.make_async_remote_copy(
            src_ref=block, dst_ref=block,
            send_sem=ss.at[d, h, s - 1], recv_sem=rr.at[d, h, s - 1],
            device_id={"seq": neighbour[d]}, device_id_type=MESH,
        ).wait_recv()

    def gather_finish(buf, ss, rr, h):
        for d in range(2):
            if carries(h, d):
                gather_wait(buf, ss, rr, h, half, d)
            elif half > 1:
                gather_wait(buf, ss, rr, h, half - 1, d)

    def rs_copy(h, s, d):
        return pltpu.make_async_remote_copy(
            src_ref=rs_out.at[d, h, s - 1], dst_ref=rs_in.at[d, h, s - 1],
            send_sem=rs_s.at[d, h, s - 1], recv_sem=rs_r.at[d, h, s - 1],
            device_id={"seq": neighbour[d]}, device_id_type=MESH,
        )

    def reduce_send(h, s):
        for d in range(2):
            if s == 1 and not carries(h, d):
                continue
            target = at_pos(pos + sign[d] * (half - s + 1))
            part = pg[h, target]
            if s > 2 or (s == 2 and carries(h, d)):
                rs_copy(h, s - 1, d).wait_recv()
                part = part + rs_in[d, h, s - 2].astype(F32)
            rs_out[d, h, s - 1] = part.astype(BF16)
            c = rs_copy(h, s, d)
            c.start()
            sent.append(c)

    def reduce_finish(h):
        total = pg[h, me]
        for d in range(2):
            if half > 1 or carries(h, d):
                rs_copy(h, half, d).wait_recv()
                total = total + rs_in[d, h, half - 1].astype(F32)
        for m, w in enumerate((w1, w3, w2)):
            upd = w[h] + total[m]
            own[h, m] = upd
            ug[h, me, m] = upd.astype(BF16)

    def cols(h):
        return slice(h * hd, (h + 1) * hd)

    halo = []
    for h in range(heads):
        for j, (src, dst) in enumerate(((k, kx), (v, vx))):
            halo.append(pltpu.make_async_remote_copy(
                src_ref=src.at[rows - WINDOW:rows, cols(h)], dst_ref=dst.at[0:WINDOW, cols(h)],
                send_sem=halo_s.at[h, j], recv_sem=halo_r.at[h, j],
                device_id={"seq": after}, device_id_type=MESH,
            ))

    def halo_send(h):
        @pl.when(me < n - 1)
        def _():
            for j in range(2):
                halo[2 * h + j].start()

    def halo_wait(h):
        @pl.when(me > 0)
        def _():
            for j in range(2):
                halo[2 * h + j].wait_recv()

    def column(row):
        return jnp.transpose(jnp.broadcast_to(row, (TILE, row.shape[1])))

    def prepare(h):
        eta = column(rate[h:h + 1, :])[:, :1]
        gv[h] = (eta * v[:, cols(h)].astype(F32)).astype(BF16)

    def full(buf, h, m):
        return buf[h, :, m].reshape(n * shard, hd)

    def tiles(body):
        @pl.loop(0, rows // TILE)
        def _(i):
            body(pl.ds(pl.multiple_of(i * TILE, TILE), TILE))

    def gradients(h):
        @tiles
        def _(at):
            kt, gt = k[at, cols(h)], gv[h, at]
            a = dot(kt, full(wg, h, 0))
            b = dot(kt, full(wg, h, 1))
            back = dot_rhs_t(gt, full(wg, h, 2))
            g = jax.nn.sigmoid(a)
            ag = a * g
            hid[at, :] = (ag * b).astype(BF16)
            dab[at, :fast] = (back * b * g * (1.0 + a * (1.0 - g))).astype(BF16)
            dab[at, fast:] = (back * ag).astype(BF16)

        kh = k[:, cols(h)]
        for m in range(2):
            pg[h, :, m] = dot_lhs_t(kh, dab[:, m * fast:(m + 1) * fast]).reshape(n, shard, fast)
        pg[h, :, 2] = dot_lhs_t(hid[...], gv[h]).reshape(n, shard, hd)

    def attention(h):
        span = WINDOW + TILE
        @pl.loop(0, rows // TILE)
        def _(i):
            start = pl.multiple_of(i * TILE, TILE)
            s = dot_rhs_t(q[pl.ds(start, TILE), cols(h)], kx[pl.ds(start, span), cols(h)])
            s = s * (1.0 / math.sqrt(hd))
            r = lax.broadcasted_iota(jnp.int32, (TILE, span), 0)
            c = lax.broadcasted_iota(jnp.int32, (TILE, span), 1)
            ok = (c > r) & (c <= r + WINDOW) & (start + c + me * rows >= WINDOW)
            s = jnp.where(ok, s, -jnp.inf)
            e = jnp.exp(s - jnp.max(s, axis=1, keepdims=True))
            p = (e * (1.0 / jnp.sum(e, axis=1, keepdims=True))).astype(BF16)
            attn[h, pl.ds(start, TILE), :] = dot(p, vx[pl.ds(start, span), cols(h)])

    def sum_squares(buf, h, m):
        x = full(buf, h, m).astype(F32)
        return jnp.sum(x * x, axis=0, keepdims=True)

    def apply(h):
        ratio = []
        for m, out in enumerate((o1, o3, o2)):
            old, new = sum_squares(wg, h, m), sum_squares(ug, h, m)
            ratio.append(jnp.sqrt(old) / jnp.sqrt(new + EPS))
            out[h] = own[h, m] * ratio[m]

        @tiles
        def _(at):
            qt = q[at, cols(h)]
            a = dot(qt, full(ug, h, 0)) * ratio[0]
            b = dot(qt, full(ug, h, 1)) * ratio[1]
            hh = (a * jax.nn.sigmoid(a) * b).astype(BF16)
            f = dot(hh, full(ug, h, 2)) * ratio[2]
            branch[h, at, :] = f
            row_sq = jnp.broadcast_to(jnp.sum(f * f, axis=1, keepdims=True), (TILE, TILE))
            flat = jnp.transpose(row_sq)[:8]
            if h == 0:
                sq[:, at] = flat
            else:
                sq[:, at] = sq[:, at] + flat

    for h in range(heads):
        gather_send(wg, ag_s, ag_r, h, 1)
    for src, dst in ((k, kx), (v, vx)):
        dst[WINDOW:, :] = src[...]

    @pl.when(me == 0)
    def _():
        for dst in (kx, vx):
            dst[:WINDOW, :] = jnp.zeros((WINDOW, width), BF16)

    for h in range(heads):
        prepare(h)
    for s in range(2, half + 1):
        for h in range(heads):
            gather_send(wg, ag_s, ag_r, h, s)
    halo_send(0)
    for h in range(heads):
        gather_finish(wg, ag_s, ag_r, h)
        gradients(h)
        reduce_send(h, 1)
    halo_wait(0)
    for h in range(heads):
        if h > 0:
            halo_send(h)
    for s in range(2, half + 1):
        for h in range(heads):
            reduce_send(h, s)
        if s == 2:
            attention(0)
    for h in range(heads):
        reduce_finish(h)
        gather_send(ug, au_s, au_r, h, 1)
    for h in range(1, heads):
        halo_wait(h)
        attention(h)
    for s in range(2, half + 1):
        for h in range(heads):
            gather_send(ug, au_s, au_r, h, s)
    for h in range(heads):
        gather_finish(ug, au_s, au_r, h)
        apply(h)

    mine = []
    for d in range(1, hn):
        c = pltpu.make_async_remote_copy(
            src_ref=sq, dst_ref=sq_in.at[d - 1],
            send_sem=sq_s.at[d - 1], recv_sem=sq_r.at[d - 1],
            device_id={"head": lax.rem(hme + d, hn)}, device_id_type=MESH,
        )
        c.start()
        mine.append(c)
    for c in sent:
        c.wait_send()

    @pl.when(me < n - 1)
    def _():
        for c in halo:
            c.wait_send()

    total = sq[...]
    for d, c in enumerate(mine):
        c.wait_recv()
        total = total + sq_in[d]
    for c in mine:
        c.wait_send()
    sq[...] = lax.rsqrt(total * (1.0 / (hn * width)) + EPS)

    @tiles
    def _(at):
        inv = column(sq[0:1, at])[:, :1]
        for h in range(heads):
            f = branch[h, at, :] * inv * gain[:, cols(h)]
            mixed[at, cols(h)] = (attn[h, at, :] + f).astype(BF16)


def local(n, hn, queries, keys, values, rate, fast_gate, fast_up, fast_down, out_gain):
    rows, width = queries.shape
    heads, shard, hd = fast_gate.shape
    half = n // 2
    piece = (3, shard, hd)
    dma = pltpu.SemaphoreType.DMA
    vmem = pl.BlockSpec(memory_space=pltpu.VMEM)
    return pl.pallas_call(
        functools.partial(kernel, n, hn),
        out_shape=(
            jax.ShapeDtypeStruct((rows, width), BF16),
            jax.ShapeDtypeStruct(fast_gate.shape, F32),
            jax.ShapeDtypeStruct(fast_up.shape, F32),
            jax.ShapeDtypeStruct(fast_down.shape, F32),
        ),
        in_specs=[vmem] * 8,
        out_specs=(vmem,) * 4,
        scratch_shapes=[
            pltpu.VMEM((heads, n) + piece, BF16),
            pltpu.VMEM((heads, n) + piece, BF16),
            pltpu.VMEM((heads, n) + piece, F32),
            pltpu.VMEM((2, heads, half) + piece, BF16),
            pltpu.VMEM((2, heads, half) + piece, BF16),
            pltpu.VMEM((heads,) + piece, F32),
            pltpu.VMEM((WINDOW + rows, width), BF16),
            pltpu.VMEM((WINDOW + rows, width), BF16),
            pltpu.VMEM((heads, rows, hd), BF16),
            pltpu.VMEM((rows, hd), BF16),
            pltpu.VMEM((rows, 2 * hd), BF16),
            pltpu.VMEM((heads, rows, hd), F32),
            pltpu.VMEM((heads, rows, hd), F32),
            pltpu.VMEM((8, rows), F32),
            pltpu.VMEM((hn - 1, 8, rows), F32),
        ]
        + [dma((2, heads, half))] * 6
        + [dma((heads, 2))] * 2
        + [dma((hn - 1,))] * 2,
        compiler_params=pltpu.CompilerParams(
            collective_id=0, has_side_effects=True, vmem_limit_bytes=60 * 1024 * 1024
        ),
        name="ttt_layer",
    )(queries, keys, values, rate, out_gain.reshape(1, width), fast_gate, fast_up, fast_down)


def solution(mesh):
    weights = P("head", "seq", None)
    tokens = P("seq", "head")
    return jax.shard_map(
        functools.partial(local, mesh.shape["seq"], mesh.shape["head"]),
        mesh=mesh,
        in_specs=(tokens, tokens, tokens, P("head", "seq"), weights, weights, weights, P("head")),
        out_specs=(tokens, weights, weights, weights),
        check_vma=False,
    )
```

time: 460 us -> 159 us (0.35)
  waiting for transfers between devices: 361 us -> 0 us
  Pallas kernels: 0 us -> 153 us
  matrix products: 26.7 us -> 0 us
  local copies, waits for them, and re-layouts: 29.8 us -> 5.1 us
  other arithmetic: 13.4 us -> 0 us
  between operations: 14 us -> 0.65 us
  starting transfers between devices: 8.08 us -> 0 us
  blocking collectives: 6.21 us -> 0 us
    psum x1 -> x0, waiting for transfers between devices: 172 us -> none  [local(): lax.psum((grad_one, grad_three, grad_two), 'seq')]
    pallas_call x0 -> x1, Pallas kernels: none -> 153 us  [local(): pl.pallas_call(functools.partial(kernel, n, hn), out_shape=(jax.ShapeDtyp...]
    all_gather x3 -> x0, waiting for transfers between devices: 135 us -> none  [the longest x1 49 us: local(): lax.all_gather(fast_gate, 'seq', axis=1, tiled=True)]
    ppermute x2 -> x0, waiting for transfers between devices: 53.1 us -> none  [from_behind(): return lax.ppermute(block, axis, route)]
    dot_general x10 -> x0, matrix products: 26.7 us -> none  [the longest x1 5.38 us: local(): jnp.einsum('thf,hfd->thd', apply_h, use_two, preferred_element_type=jnp.f...]
    unnamed x43 -> x10, local copies, waits for them, and re-layouts: 15.8 us -> 5.1 us
    ppermute x2 -> x0, starting transfers between devices: 7.92 us -> none  [from_behind(): return lax.ppermute(block, axis, route)]
    all_gather x2 -> x0, local copies, waits for them, and re-layouts: 6.86 us -> none  [the longest x1 4.11 us: local(): lax.all_gather(fast_up, 'seq', axis=1, tiled=True)]
  transfers between devices with their start and end apart: 6 -> 0, of which waited for: 6 -> 0; matrix products, arithmetic and copies ran while one was open for 7% -> 0% of each run, Pallas kernels for 0% -> 0%
where the time goes in v1:
time: 159 us; the launch traced here: 158 us
  Pallas kernels  153 us (96%)
  local copies, waits for them, and re-layouts  5.1 us (3%)
    pallas_call x1, Pallas kernels, local(): pl.pallas_call(functools.partial(kernel, n, hn), out_shape=(jax.ShapeDtyp...  153 us
    unnamed x10, local copies, waits for them, and re-layouts  5.1 us

profile of v1, /device:TPU:0, one launch (start us, length us, event | category | flops | bytes accessed | tf_op | source)
XLA Modules:
  0.0 158.3 jit_solution(1844636624186951392)
XLA Ops:
  0.6 152.6 %ttt_layer.1 = (bf16[512,1024]{1,0:T(8,128)(2,1)}, f32[2,64,512]{2,1,0:T(8,128)}, f32[2,64,512]{2,1,0:T(8,128)}, f32[2,64,512]{2,1,0:T(8,128)}) custom-call(bf16[512,1024]{1,0:T(8,128)(2,1)} %q.1, bf16[512,1024]{1,0:T(8,128)(2,1)} %k.1, bf16[512,1024]{1,0:T(8,128)(2,1)} %v.1, f32[2,512]{1,0:T(2,128)} %rate.1, f32[1,1024]{1,0:T(1,128)} %bitcast.1, ...), custom_call_target="tpu_custom_call" | custom-call | tf_op jit(solution)/shard_map/ttt_layer/pallas_call | solution.py:317
  153.2 0.0 copy-start.2
  153.2 2.3 %copy.16 = bf16[512,1024]{1,0:T(8,128)(2,1)} copy(bf16[512,1024]{1,0:T(8,128)(2,1)} %get-tuple-element.8) | data formatting | bytes 2097152
  155.5 0.0 copy-done.2
  155.5 0.0 copy-start.1
  155.6 0.7 copy.17
  156.3 0.3 copy-done.1
  156.6 0.0 copy-start
  156.6 0.7 copy.18
  157.3 0.3 copy-done
  157.6 0.7 copy.19
Async XLA Ops:
  153.2 2.3 %copy-start.2 = (f32[2,64,512]{2,1,0:T(8,128)S(1)}, f32[2,64,512]{2,1,0:T(8,128)}, u32[]{:S(2)}) copy-start(f32[2,64,512]{2,1,0:T(8,128)} %get-tuple-element.9) | copy-start | bytes 786436
  155.5 1.0 copy-start.1
  156.6 1.0 copy-start

commit v2 on v0

v2 whole, which is shorter than its diff:
```python
import functools
import math

import jax
import jax.numpy as jnp
from jax import lax
from jax.experimental import pallas as pl
from jax.experimental.pallas import tpu as pltpu
from jax.sharding import PartitionSpec as P

WINDOW = 512
EPS = 1e-06
TILE = 128
MESH = pl.DeviceIdType.MESH
F32 = jnp.float32
BF16 = jnp.bfloat16


def dot(a, b):
    return jnp.dot(a, b, preferred_element_type=F32)


def dot_lhs_t(a, b):
    return lax.dot_general(a, b, (((0,), (0,)), ((), ())), preferred_element_type=F32)


def dot_rhs_t(a, b):
    return lax.dot_general(a, b, (((1,), (1,)), ((), ())), preferred_element_type=F32)


def kernel(
    n, hn,
    q, k, v, rate, gain, w1, w3, w2,
    mixed, o1, o3, o2,
    wg, ug, pg, rs_out, rs_in, wb_out, wf_out, wf_in, own, g_out, g_in, ratio_out, ratio_in,
    qx, kx, vx, eta_x, gv, hid, dab, attn, attn_out, attn_in, branch, f_out, f_in, sq, sq_in,
    ag_s, ag_r, rs_s, rs_r, au_s, au_r, x_s, x_r, halo_s, halo_r, f_s, f_r, sq_s, sq_r,
):
    rows, width = q.shape
    heads, shard, hd = w1.shape
    line = n // 2
    tiles = rows // TILE
    me = lax.axis_index("seq")
    hme = lax.axis_index("head")
    m = lax.div(me, 2)
    c = lax.rem(me, 2)
    oc = 1 - c
    partner = 2 * m + oc
    step_to = (1, -1)
    weights = (w1, w3, w2)

    def seq_at(b):
        return 2 * lax.rem(b + line, line) + c

    def lanes(i):
        return pl.ds(pl.multiple_of(i * hd, hd), hd)

    def block(i):
        return pl.ds(pl.multiple_of(i * rows, rows), rows)

    def after_halo(i):
        return pl.ds(pl.multiple_of(WINDOW + i * rows, TILE), rows)

    barrier = pltpu.get_barrier_semaphore()
    for s in (partner, seq_at(m + 1), seq_at(m - 1)):
        pl.semaphore_signal(barrier, inc=1, device_id={"seq": s}, device_id_type=MESH)
    for d in range(1, hn):
        pl.semaphore_signal(
            barrier, inc=1, device_id={"head": lax.rem(hme + d, hn)}, device_id_type=MESH
        )
    for j, w in enumerate(weights):
        wg[j, m, c] = w[c].astype(BF16)
        wb_out[j] = w[oc].astype(BF16)
        wf_out[j] = w[oc]
    pl.semaphore_wait(barrier, 3 + hn - 1)

    pending = []

    def start(copy, when=None):
        if when is None:
            copy.start()
        else:
            pl.when(when)(copy.start)
        pending.append((copy, when))

    def wait(copy, when):
        pl.when(when)(copy.wait_recv)

    def to_partner(i, src, dst):
        return pltpu.make_async_remote_copy(
            src_ref=src, dst_ref=dst, send_sem=x_s.at[i], recv_sem=x_r.at[i],
            device_id={"seq": partner}, device_id_type=MESH,
        )

    x_w = to_partner(0, wb_out, wg.at[:, m, c])
    x_k = to_partner(1, k.at[:, lanes(oc)], kx.at[after_halo(c)])
    x_v = to_partner(2, v.at[:, lanes(oc)], vx.at[after_halo(c)])
    x_e = to_partner(3, rate, eta_x.at[c])
    x_f = to_partner(4, wf_out, wf_in)
    x_q = to_partner(5, q.at[:, lanes(oc)], qx.at[block(c)])
    x_g = to_partner(6, g_out, g_in)
    x_a = to_partner(7, attn_out, attn_in)
    x_r_ = to_partner(8, ratio_out, ratio_in)
    for x in (x_w, x_k, x_v, x_e, x_f, x_q):
        start(x)

    def link(ss, rr, src, dst, d, j, s):
        return pltpu.make_async_remote_copy(
            src_ref=src, dst_ref=dst, send_sem=ss.at[d, j, s - 1], recv_sem=rr.at[d, j, s - 1],
            device_id={"seq": seq_at(m + step_to[d])}, device_id_type=MESH,
        )

    def ahead(d):
        return line - 1 - m if d == 0 else m

    def gather_copy(buf, ss, rr, d, j, s):
        b = lax.rem(m - step_to[d] * (s - 1) + line, line)
        return link(ss, rr, buf.at[j, b], buf.at[j, b], d, j, s)

    def gather_wait(buf, ss, rr, d, j, s):
        b = lax.rem(m - step_to[d] * s + line, line)
        wait(link(ss, rr, buf.at[j, b], buf.at[j, b], d, j, s), ahead(1 - d) >= s)

    def gather_send(buf, ss, rr, j, s):
        for d in range(2):
            if s > 1:
                gather_wait(buf, ss, rr, d, j, s - 1)
            start(
                gather_copy(buf, ss, rr, d, j, s),
                jnp.logical_and(ahead(d) >= 1, ahead(1 - d) >= s - 1),
            )

    def gather_finish(buf, ss, rr, j):
        for d in range(2):
            gather_wait(buf, ss, rr, d, j, line - 1)

    def reduce_copy(d, j, s):
        return link(rs_s, rs_r, rs_out.at[d, j, s - 1], rs_in.at[d, j, s - 1], d, j, s)

    def reduce_send(j, s):
        for d in range(2):
            target = line - s if d == 0 else s - 1
            copy = reduce_copy(d, j, s)
            active = target > m if d == 0 else target < m
            first = ahead(1 - d) == 0

            @pl.when(jnp.logical_and(active, first))
            def _():
                rs_out[d, j, s - 1] = pg[j, target].astype(BF16)

            @pl.when(jnp.logical_and(active, jnp.logical_not(first)))
            def _():
                copy.wait_recv()
                part = pg[j, target] + rs_in[d, j, s - 1].astype(F32)
                rs_out[d, j, s - 1] = part.astype(BF16)

            start(copy, active)

    def reduce_finish(j):
        own[j] = pg[j, m]
        for d in range(2):
            for s in range(1, line):
                target = line - s if d == 0 else s - 1

                @pl.when(target == m)
                def _():
                    reduce_copy(d, j, s).wait_recv()
                    own[j] = own[j] + rs_in[d, j, s - 1].astype(F32)

        g_out[j] = own[j, oc]
        upd = own[j, c] + weights[j][c]
        own[j, c] = upd
        ug[j, m, c] = upd.astype(BF16)
        ug[j, m, oc] = (own[j, oc] + wf_in[j]).astype(BF16)

    halo = [
        pltpu.make_async_remote_copy(
            src_ref=x.at[2 * rows:2 * rows + WINDOW], dst_ref=x.at[0:WINDOW],
            send_sem=halo_s.at[i], recv_sem=halo_r.at[i],
            device_id={"seq": seq_at(m + 1)}, device_id_type=MESH,
        )
        for i, x in enumerate((kx, vx))
    ]

    def column(row):
        return jnp.transpose(jnp.broadcast_to(row, (TILE, row.shape[1])))

    def full(buf, j):
        return buf[j].reshape(n * shard, hd)

    def gradients():
        @pl.loop(0, 2 * tiles)
        def _(i):
            at = pl.ds(pl.multiple_of(i * TILE, TILE), TILE)
            kt = kx[pl.ds(pl.multiple_of(WINDOW + i * TILE, TILE), TILE), :]
            gt = gv[at, :]
            a = dot(kt, full(wg, 0))
            b = dot(kt, full(wg, 1))
            back = dot_rhs_t(gt, full(wg, 2))
            g = jax.nn.sigmoid(a)
            ag = a * g
            hid[at, :] = (ag * b).astype(BF16)
            dab[0, at, :] = (back * b * g * (1.0 + a * (1.0 - g))).astype(BF16)
            dab[1, at, :] = (back * ag).astype(BF16)

    def product(j):
        if j == 2:
            g = dot_lhs_t(hid[...], gv[...])
        else:
            g = dot_lhs_t(kx[WINDOW:, :], dab[j])
        pg[j] = g.reshape(line, 2, shard, hd)

    def attention(b, out):
        span = WINDOW + TILE

        @pl.loop(0, tiles)
        def _(i):
            base = pl.multiple_of(b * rows + i * TILE, TILE)
            s = dot_rhs_t(qx[pl.ds(base, TILE), :], kx[pl.ds(base, span), :])
            s = s * (1.0 / math.sqrt(hd))
            r = lax.broadcasted_iota(jnp.int32, (TILE, span), 0)
            u = lax.broadcasted_iota(jnp.int32, (TILE, span), 1)
            ok = (u > r) & (u <= r + WINDOW) & (base + u + m * 2 * rows >= WINDOW)
            s = jnp.where(ok, s, -jnp.inf)
            e = jnp.exp(s - jnp.max(s, axis=1, keepdims=True))
            p = (e * (1.0 / jnp.sum(e, axis=1, keepdims=True))).astype(BF16)
            res = dot(p, vx[pl.ds(base, span), :])
            out[pl.ds(pl.multiple_of(i * TILE, TILE), TILE), :] = res.astype(out.dtype)

    def sum_squares(buf, j):
        x = full(buf, j).astype(F32)
        return jnp.sum(x * x, axis=0, keepdims=True)

    def f_copy(i):
        at = pl.ds(pl.multiple_of(i * TILE, TILE), TILE)
        return pltpu.make_async_remote_copy(
            src_ref=f_out.at[at], dst_ref=f_in.at[at], send_sem=f_s.at[i], recv_sem=f_r.at[i],
            device_id={"seq": partner}, device_id_type=MESH,
        )

    def flat(f):
        row_sq = jnp.broadcast_to(jnp.sum(f * f, axis=1, keepdims=True), (TILE, TILE))
        return jnp.transpose(row_sq)[:8]

    def apply_tile(i, b):
        qt = qx[pl.ds(pl.multiple_of(b * rows + i * TILE, TILE), TILE), :]
        a = dot(qt, full(ug, 0)) * ratio_out[0:1]
        g = dot(qt, full(ug, 1)) * ratio_out[1:2]
        hh = (a * jax.nn.sigmoid(a) * g).astype(BF16)
        return dot(hh, full(ug, 2)) * ratio_out[2:3]

    kx[after_halo(c), :] = k[:, lanes(c)]
    vx[after_halo(c), :] = v[:, lanes(c)]
    qx[block(c), :] = q[:, lanes(c)]
    eta_x[c] = rate[...]

    @pl.when(m == 0)
    def _():
        for dst in (kx, vx):
            dst[:WINDOW, :] = jnp.zeros((WINDOW, hd), BF16)

    order_w, order_g = (0, 1, 2), (2, 0, 1)
    x_w.wait_recv()
    for j in order_w:
        gather_send(wg, ag_s, ag_r, j, 1)
    for s in range(2, line):
        for j in order_w:
            gather_send(wg, ag_s, ag_r, j, s)
    for x in (x_k, x_v, x_e):
        x.wait_recv()
    for h in halo:
        start(h, m < line - 1)
    for b in range(2):
        eta = column(eta_x[b, pl.ds(c, 1), :])[:, :1]
        at = slice(b * rows, (b + 1) * rows)
        vb = vx[WINDOW + b * rows:WINDOW + (b + 1) * rows, :]
        gv[at, :] = (eta * vb.astype(F32)).astype(BF16)
    for j in order_w:
        gather_finish(wg, ag_s, ag_r, j)
    gradients()
    for j in order_g:
        product(j)
        reduce_send(j, 1)
    x_q.wait_recv()
    for h in halo:
        wait(h, m > 0)
    attention(oc, attn_out)
    start(x_a)
    for s in range(2, line):
        for j in order_g:
            reduce_send(j, s)
    x_f.wait_recv()
    for j in order_g:
        reduce_finish(j)
        gather_send(ug, au_s, au_r, j, 1)
    start(x_g)
    attention(c, attn)
    for j in range(3):
        ratio_out[j:j + 1] = jnp.sqrt(sum_squares(wg, j))
    for s in range(2, line):
        for j in order_g:
            gather_send(ug, au_s, au_r, j, s)
    for j in order_g:
        gather_finish(ug, au_s, au_r, j)
        ratio_out[j:j + 1] = ratio_out[j:j + 1] / jnp.sqrt(sum_squares(ug, j) + EPS)
    start(x_r_)

    @pl.loop(0, tiles)
    def _(i):
        f_out[pl.ds(pl.multiple_of(i * TILE, TILE), TILE), :] = apply_tile(i, oc).astype(BF16)
        f_copy(i).start()

    @pl.loop(0, tiles)
    def _(i):
        at = pl.ds(pl.multiple_of(i * TILE, TILE), TILE)
        f = apply_tile(i, c)
        branch[at, :] = f
        sq[:, at] = flat(f)

    x_r_.wait_recv()
    x_g.wait_recv()
    for j, (w, out) in enumerate(zip(weights, (o1, o3, o2))):
        out[c] = own[j, c] * ratio_out[j:j + 1]
        out[oc] = (w[oc] + g_in[j]) * ratio_in[j:j + 1]

    @pl.loop(0, tiles)
    def _(i):
        at = pl.ds(pl.multiple_of(i * TILE, TILE), TILE)
        f_copy(i).wait_recv()
        sq[:, at] = sq[:, at] + flat(f_in[at, :].astype(F32))

    mine = []
    for d in range(1, hn):
        copy = pltpu.make_async_remote_copy(
            src_ref=sq, dst_ref=sq_in.at[d - 1],
            send_sem=sq_s.at[d - 1], recv_sem=sq_r.at[d - 1],
            device_id={"head": lax.rem(hme + d, hn)}, device_id_type=MESH,
        )
        copy.start()
        mine.append(copy)
    for copy, when in pending:
        if when is None:
            copy.wait_send()
        else:
            pl.when(when)(copy.wait_send)

    @pl.loop(0, tiles)
    def _(i):
        f_copy(i).wait_send()

    x_a.wait_recv()
    total = sq[...]
    for d, copy in enumerate(mine):
        copy.wait_recv()
        total = total + sq_in[d]
    for copy in mine:
        copy.wait_send()
    sq[...] = lax.rsqrt(total * (1.0 / (hn * width)) + EPS)

    @pl.loop(0, tiles)
    def _(i):
        at = pl.ds(pl.multiple_of(i * TILE, TILE), TILE)
        inv = column(sq[0:1, at])[:, :1]
        mixed[at, lanes(c)] = (attn[at, :] + branch[at, :] * inv * gain[:, lanes(c)]).astype(BF16)
        other = f_in[at, :].astype(F32) * inv * gain[:, lanes(oc)]
        mixed[at, lanes(oc)] = (attn_in[at, :].astype(F32) + other).astype(BF16)


def local(n, hn, queries, keys, values, rate, fast_gate, fast_up, fast_down, out_gain):
    rows, width = queries.shape
    heads, shard, hd = fast_gate.shape
    line = n // 2
    piece = (3, shard, hd)
    dma = pltpu.SemaphoreType.DMA
    vmem = pl.BlockSpec(memory_space=pltpu.VMEM)
    return pl.pallas_call(
        functools.partial(kernel, n, hn),
        out_shape=(
            jax.ShapeDtypeStruct((rows, width), BF16),
            jax.ShapeDtypeStruct(fast_gate.shape, F32),
            jax.ShapeDtypeStruct(fast_up.shape, F32),
            jax.ShapeDtypeStruct(fast_down.shape, F32),
        ),
        in_specs=[vmem] * 8,
        out_specs=(vmem,) * 4,
        scratch_shapes=[
            pltpu.VMEM((3, line, 2, shard, hd), BF16),
            pltpu.VMEM((3, line, 2, shard, hd), BF16),
            pltpu.VMEM((3, line, 2, shard, hd), F32),
            pltpu.VMEM((2, 3, line - 1, 2, shard, hd), BF16),
            pltpu.VMEM((2, 3, line - 1, 2, shard, hd), BF16),
            pltpu.VMEM(piece, BF16),
            pltpu.VMEM(piece, F32),
            pltpu.VMEM(piece, F32),
            pltpu.VMEM((3, 2, shard, hd), F32),
            pltpu.VMEM(piece, F32),
            pltpu.VMEM(piece, F32),
            pltpu.VMEM((8, hd), F32),
            pltpu.VMEM((8, hd), F32),
            pltpu.VMEM((2 * rows, hd), BF16),
            pltpu.VMEM((WINDOW + 2 * rows, hd), BF16),
            pltpu.VMEM((WINDOW + 2 * rows, hd), BF16),
            pltpu.VMEM((2,) + rate.shape, F32),
            pltpu.VMEM((2 * rows, hd), BF16),
            pltpu.VMEM((2 * rows, hd), BF16),
            pltpu.VMEM((2, 2 * rows, hd), BF16),
            pltpu.VMEM((rows, hd), F32),
            pltpu.VMEM((rows, hd), BF16),
            pltpu.VMEM((rows, hd), BF16),
            pltpu.VMEM((rows, hd), F32),
            pltpu.VMEM((rows, hd), BF16),
            pltpu.VMEM((rows, hd), BF16),
            pltpu.VMEM((8, rows), F32),
            pltpu.VMEM((hn - 1, 8, rows), F32),
        ]
        + [dma((2, 3, line - 1))] * 6
        + [dma((9,))] * 2
        + [dma((2,))] * 2
        + [dma((rows // TILE,))] * 2
        + [dma((hn - 1,))] * 2,
        compiler_params=pltpu.CompilerParams(
            collective_id=0, has_side_effects=True, vmem_limit_bytes=60 * 1024 * 1024
        ),
        name="ttt_layer",
    )(queries, keys, values, rate, out_gain.reshape(1, width), fast_gate, fast_up, fast_down)


def solution(mesh):
    weights = P("head", "seq", None)
    tokens = P("seq", "head")
    return jax.shard_map(
        functools.partial(local, mesh.shape["seq"], mesh.shape["head"]),
        mesh=mesh,
        in_specs=(tokens, tokens, tokens, P("head", "seq"), weights, weights, weights, P("head")),
        out_specs=(tokens, weights, weights, weights),
        check_vma=False,
    )
```

time: 460 us -> 141 us (0.31)
  waiting for transfers between devices: 361 us -> 0 us
  Pallas kernels: 0 us -> 135 us
  matrix products: 26.7 us -> 0 us
  local copies, waits for them, and re-layouts: 29.8 us -> 5.1 us
  other arithmetic: 13.4 us -> 0 us
  between operations: 14 us -> 0.65 us
  starting transfers between devices: 8.08 us -> 0 us
  blocking collectives: 6.21 us -> 0 us
    psum x1 -> x0, waiting for transfers between devices: 172 us -> none  [local(): lax.psum((grad_one, grad_three, grad_two), 'seq')]
    all_gather x3 -> x0, waiting for transfers between devices: 135 us -> none  [the longest x1 49 us: local(): lax.all_gather(fast_gate, 'seq', axis=1, tiled=True)]
    pallas_call x0 -> x1, Pallas kernels: none -> 135 us  [local(): pl.pallas_call(functools.partial(kernel, n, hn), out_shape=(jax.ShapeDtyp...]
    ppermute x2 -> x0, waiting for transfers between devices: 53.1 us -> none  [from_behind(): return lax.ppermute(block, axis, route)]
    dot_general x10 -> x0, matrix products: 26.7 us -> none  [the longest x1 5.38 us: local(): jnp.einsum('thf,hfd->thd', apply_h, use_two, preferred_element_type=jnp.f...]
    unnamed x43 -> x10, local copies, waits for them, and re-layouts: 15.8 us -> 5.1 us
    ppermute x2 -> x0, starting transfers between devices: 7.92 us -> none  [from_behind(): return lax.ppermute(block, axis, route)]
    all_gather x2 -> x0, local copies, waits for them, and re-layouts: 6.86 us -> none  [the longest x1 4.11 us: local(): lax.all_gather(fast_up, 'seq', axis=1, tiled=True)]
  transfers between devices with their start and end apart: 6 -> 0, of which waited for: 6 -> 0; matrix products, arithmetic and copies ran while one was open for 7% -> 0% of each run, Pallas kernels for 0% -> 0%
where the time goes in v2:
time: 141 us
  Pallas kernels  135 us (96%)
  local copies, waits for them, and re-layouts  5.1 us (4%)
    pallas_call x1, Pallas kernels, local(): pl.pallas_call(functools.partial(kernel, n, hn), out_shape=(jax.ShapeDtyp...  135 us
    unnamed x10, local copies, waits for them, and re-layouts  5.1 us

profile of v2, /device:TPU:0, one launch (start us, length us, event | category | flops | bytes accessed | tf_op | source)
XLA Modules:
  0.0 141.0 jit_solution(3748269822891473504)
XLA Ops:
  0.6 135.2 %ttt_layer.1 = (bf16[512,1024]{1,0:T(8,128)(2,1)}, f32[2,64,512]{2,1,0:T(8,128)}, f32[2,64,512]{2,1,0:T(8,128)}, f32[2,64,512]{2,1,0:T(8,128)}) custom-call(bf16[512,1024]{1,0:T(8,128)(2,1)} %q.1, bf16[512,1024]{1,0:T(8,128)(2,1)} %k.1, bf16[512,1024]{1,0:T(8,128)(2,1)} %v.1, f32[2,512]{1,0:T(2,128)} %rate.1, f32[1,1024]{1,0:T(1,128)} %bitcast.1, ...), custom_call_target="tpu_custom_call" | custom-call | tf_op jit(solution)/shard_map/ttt_layer/pallas_call | solution.py:376
  135.9 0.0 copy-start.2
  135.9 2.3 %copy.16 = bf16[512,1024]{1,0:T(8,128)(2,1)} copy(bf16[512,1024]{1,0:T(8,128)(2,1)} %get-tuple-element.8) | data formatting | bytes 2097152
  138.2 0.0 copy-done.2
  138.2 0.0 copy-start.1
  138.2 0.7 copy.17
  138.9 0.3 copy-done.1
  139.2 0.0 copy-start
  139.2 0.7 copy.18
  139.9 0.3 copy-done
  140.3 0.7 copy.19
Async XLA Ops:
  135.9 2.3 %copy-start.2 = (f32[2,64,512]{2,1,0:T(8,128)S(1)}, f32[2,64,512]{2,1,0:T(8,128)}, u32[]{:S(2)}) copy-start(f32[2,64,512]{2,1,0:T(8,128)} %get-tuple-element.9) | copy-start | bytes 786436
  138.2 1.0 copy-start.1
  139.2 1.0 copy-start

commit v3 on v2

--- a/solution.py
+++ b/solution.py
@@ -137,16 +137,19 @@
     def reduce_copy(d, j, s):
         return link(rs_s, rs_r, rs_out.at[d, j, s - 1], rs_in.at[d, j, s - 1], d, j, s)
 
-    def reduce_send(j, s):
+    def reduce_send(j, s, near):
         for d in range(2):
             target = line - s if d == 0 else s - 1
             copy = reduce_copy(d, j, s)
-            active = target > m if d == 0 else target < m
+            closer = ahead(1 - d) * 2 < line
+            turn = closer if near else jnp.logical_not(closer)
+            active = jnp.logical_and(turn, target > m if d == 0 else target < m)
             first = ahead(1 - d) == 0
-
-            @pl.when(jnp.logical_and(active, first))
-            def _():
-                rs_out[d, j, s - 1] = pg[j, target].astype(BF16)
+            if near:
+
+                @pl.when(jnp.logical_and(active, first))
+                def _():
+                    rs_out[d, j, s - 1] = pg[j, target].astype(BF16)
 
             @pl.when(jnp.logical_and(active, jnp.logical_not(first)))
             def _():
@@ -155,6 +158,13 @@
                 rs_out[d, j, s - 1] = part.astype(BF16)
 
             start(copy, active)
+
+    def reduce_piece(j):
+        for s in range(1, line + 1):
+            if s < line:
+                reduce_send(j, s, True)
+            if s > 1:
+                reduce_send(j, s - 1, False)
 
     def reduce_finish(j):
         own[j] = pg[j, m]
@@ -259,17 +269,18 @@
         for dst in (kx, vx):
             dst[:WINDOW, :] = jnp.zeros((WINDOW, hd), BF16)
 
-    order_w, order_g = (0, 1, 2), (2, 0, 1)
+    order_w = (0, 1, 2)
     x_w.wait_recv()
     for j in order_w:
         gather_send(wg, ag_s, ag_r, j, 1)
     for s in range(2, line):
         for j in order_w:
             gather_send(wg, ag_s, ag_r, j, s)
-    for x in (x_k, x_v, x_e):
-        x.wait_recv()
-    for h in halo:
-        start(h, m < line - 1)
+    x_k.wait_recv()
+    start(halo[0], m < line - 1)
+    x_v.wait_recv()
+    start(halo[1], jnp.logical_and(m < line - 1, m * 2 < line))
+    x_e.wait_recv()
     for b in range(2):
         eta = column(eta_x[b, pl.ds(c, 1), :])[:, :1]
         at = slice(b * rows, (b + 1) * rows)
@@ -278,29 +289,44 @@
     for j in order_w:
         gather_finish(wg, ag_s, ag_r, j)
     gradients()
-    for j in order_g:
-        product(j)
-        reduce_send(j, 1)
+
+    def pass_on(j, s):
+        if s < line:
+            gather_send(ug, au_s, au_r, j, s)
+
+    product(0)
+    reduce_piece(0)
+    product(1)
+    reduce_piece(1)
+    product(2)
+    x_f.wait_recv()
+    reduce_finish(0)
+    pass_on(0, 1)
+    reduce_piece(2)
+    start(halo[1], jnp.logical_and(m < line - 1, m * 2 >= line))
+    reduce_finish(1)
+    pass_on(1, 1)
+    pass_on(0, 2)
+    reduce_finish(2)
+    pass_on(2, 1)
+    start(x_g)
+    pass_on(1, 2)
+    pass_on(0, 3)
     x_q.wait_recv()
     for h in halo:
         wait(h, m > 0)
     attention(oc, attn_out)
     start(x_a)
-    for s in range(2, line):
-        for j in order_g:
-            reduce_send(j, s)
-    x_f.wait_recv()
-    for j in order_g:
-        reduce_finish(j)
-        gather_send(ug, au_s, au_r, j, 1)
-    start(x_g)
+    pass_on(2, 2)
+    pass_on(1, 3)
     attention(c, attn)
     for j in range(3):
         ratio_out[j:j + 1] = jnp.sqrt(sum_squares(wg, j))
-    for s in range(2, line):
-        for j in order_g:
-            gather_send(ug, au_s, au_r, j, s)
-    for j in order_g:
+    pass_on(2, 3)
+    for s in range(4, line):
+        for j in order_w:
+            pass_on(j, s)
+    for j in order_w:
         gather_finish(ug, au_s, au_r, j)
         ratio_out[j:j + 1] = ratio_out[j:j + 1] / jnp.sqrt(sum_squares(ug, j) + EPS)
     start(x_r_)

time: 141 us -> 133 us (0.943)
  the two profiles are of different devices: /device:TPU:0 before, /device:TPU:25 now
where the time goes in v3:
time: 133 us
  Pallas kernels  127 us (95%)
  local copies, waits for them, and re-layouts  5.1 us (4%)
    pallas_call x1, Pallas kernels, local(): pl.pallas_call(functools.partial(kernel, n, hn), out_shape=(jax.ShapeDtyp...  127 us
    unnamed x10, local copies, waits for them, and re-layouts  5.1 us

profile of v3, /device:TPU:25, one launch (start us, length us, event | category | flops | bytes accessed | tf_op | source)
XLA Modules:
  0.0 133.2 jit_solution(2192941522060824337)
XLA Ops:
  0.6 127.5 %ttt_layer.1 = (bf16[512,1024]{1,0:T(8,128)(2,1)}, f32[2,64,512]{2,1,0:T(8,128)}, f32[2,64,512]{2,1,0:T(8,128)}, f32[2,64,512]{2,1,0:T(8,128)}) custom-call(bf16[512,1024]{1,0:T(8,128)(2,1)} %q.1, bf16[512,1024]{1,0:T(8,128)(2,1)} %k.1, bf16[512,1024]{1,0:T(8,128)(2,1)} %v.1, f32[2,512]{1,0:T(2,128)} %rate.1, f32[1,1024]{1,0:T(1,128)} %bitcast.1, ...), custom_call_target="tpu_custom_call" | custom-call | tf_op jit(solution)/shard_map/ttt_layer/pallas_call | solution.py:402
  128.1 0.0 copy-start.2
  128.1 2.3 %copy.16 = bf16[512,1024]{1,0:T(8,128)(2,1)} copy(bf16[512,1024]{1,0:T(8,128)(2,1)} %get-tuple-element.8) | data formatting | bytes 2097152
  130.4 0.0 copy-done.2
  130.4 0.0 copy-start.1
  130.4 0.7 copy.17
  131.1 0.3 copy-done.1
  131.5 0.0 copy-start
  131.5 0.7 copy.18
  132.2 0.3 copy-done
  132.5 0.7 copy.19
Async XLA Ops:
  128.1 2.3 %copy-start.2 = (f32[2,64,512]{2,1,0:T(8,128)S(1)}, f32[2,64,512]{2,1,0:T(8,128)}, u32[]{:S(2)}) copy-start(f32[2,64,512]{2,1,0:T(8,128)} %get-tuple-element.9) | copy-start | bytes 786436
  130.4 1.0 copy-start.1
  131.5 1.0 copy-start

commit v4 on v3

--- a/solution.py
+++ b/solution.py
@@ -279,7 +279,7 @@
     x_k.wait_recv()
     start(halo[0], m < line - 1)
     x_v.wait_recv()
-    start(halo[1], jnp.logical_and(m < line - 1, m * 2 < line))
+    start(halo[1], m < line - 1)
     x_e.wait_recv()
     for b in range(2):
         eta = column(eta_x[b, pl.ds(c, 1), :])[:, :1]
@@ -303,7 +303,6 @@
     reduce_finish(0)
     pass_on(0, 1)
     reduce_piece(2)
-    start(halo[1], jnp.logical_and(m < line - 1, m * 2 >= line))
     reduce_finish(1)
     pass_on(1, 1)
     pass_on(0, 2)

time: 133 us -> 126 us (0.947)
  the two profiles are of different devices: /device:TPU:25 before, /device:TPU:0 now
where the time goes in v4:
time: 126 us
  Pallas kernels  120 us (95%)
  local copies, waits for them, and re-layouts  5.1 us (4%)
    pallas_call x1, Pallas kernels, local(): pl.pallas_call(functools.partial(kernel, n, hn), out_shape=(jax.ShapeDtyp...  120 us
    unnamed x10, local copies, waits for them, and re-layouts  5.1 us

profile of v4, /device:TPU:0, one launch (start us, length us, event | category | flops | bytes accessed | tf_op | source)
XLA Modules:
  0.0 126.0 jit_solution(8546172419968905860)
XLA Ops:
  0.6 120.2 %ttt_layer.1 = (bf16[512,1024]{1,0:T(8,128)(2,1)}, f32[2,64,512]{2,1,0:T(8,128)}, f32[2,64,512]{2,1,0:T(8,128)}, f32[2,64,512]{2,1,0:T(8,128)}) custom-call(bf16[512,1024]{1,0:T(8,128)(2,1)} %q.1, bf16[512,1024]{1,0:T(8,128)(2,1)} %k.1, bf16[512,1024]{1,0:T(8,128)(2,1)} %v.1, f32[2,512]{1,0:T(2,128)} %rate.1, f32[1,1024]{1,0:T(1,128)} %bitcast.1, ...), custom_call_target="tpu_custom_call" | custom-call | tf_op jit(solution)/shard_map/ttt_layer/pallas_call | solution.py:401
  120.9 0.0 copy-start.2
  120.9 2.3 %copy.16 = bf16[512,1024]{1,0:T(8,128)(2,1)} copy(bf16[512,1024]{1,0:T(8,128)(2,1)} %get-tuple-element.8) | data formatting | bytes 2097152
  123.2 0.0 copy-done.2
  123.2 0.0 copy-start.1
  123.2 0.7 copy.17
  123.9 0.3 copy-done.1
  124.2 0.0 copy-start
  124.2 0.7 copy.18
  124.9 0.3 copy-done
  125.3 0.7 copy.19
Async XLA Ops:
  120.9 2.3 %copy-start.2 = (f32[2,64,512]{2,1,0:T(8,128)S(1)}, f32[2,64,512]{2,1,0:T(8,128)}, u32[]{:S(2)}) copy-start(f32[2,64,512]{2,1,0:T(8,128)} %get-tuple-element.9) | copy-start | bytes 786436
  123.2 1.0 copy-start.1
  124.2 1.0 copy-start
